TPU v7x, 32 devices: a whole 2x2x4 slice. The times are simulated.
32 devices in a mesh: fsdp: 2 (over x), ctx: 4 (over y, core), tp: 4 (over z).
Axes of the slice: x: 2, y: 2, z: 4, core: 2. Of those that a mesh axis runs over, the one named last changes fastest.
Arguments:
- tokens: bfloat16 [8, 512, 768], P(('fsdp', 'tp'), 'ctx'), may hold values from -6 to 6
- seg_ids: int32 [8, 512], P(('fsdp', 'tp')), may hold values from 0 to 2, never falling along the last dimension, each value on 1 to 384 neighbouring positions
- routes: int32 [8, 512, 2], P(('fsdp', 'tp'), 'ctx'), may hold values from 0 to 3, all different within a row; in each aligned block of 128 rows (0 to 127, 128 to 255, ..., all dimensions but the last counted through in order) at most 80 rows name the same one
- norm_attn: bfloat16 [768], P('fsdp'), may hold values from 0.5 to 1.5
- weight_qkv: bfloat16 [768, 2304], P('fsdp'), may hold values from -0.21875 to 0.21875
- weight_proj: bfloat16 [768, 768], P(None, 'fsdp'), may hold values from -0.875 to 0.875
- rel_table: float32 [12, 32], replicated, may hold values from -4 to 4
- norm_ffn: bfloat16 [768], P('fsdp'), may hold values from 0.5 to 1.5
- weight_router: bfloat16 [768, 4], P('fsdp'), may hold values from -0.21875 to 0.21875
- expert_up: bfloat16 [4, 768, 3072], P(None, 'fsdp', ('ctx', 'tp')), may hold values from -0.21875 to 0.21875
- expert_down: bfloat16 [4, 3072, 768], P(None, ('ctx', 'tp'), 'fsdp'), may hold values from -0.109375 to 0.109375
- cotangent: bfloat16 [8, 512, 768], P(('fsdp', 'tp'), 'ctx'), may hold values from -6 to 6
Outputs:
- output: bfloat16 [8, 512, 768], P(('fsdp', 'tp'), 'ctx')
- grad_tokens: float32 [8, 512, 768], P(('fsdp', 'tp'), 'ctx')
- grad_norm_attn: float32 [768], P('fsdp')
- grad_weight_qkv: float32 [768, 2304], P('fsdp')
- grad_weight_proj: float32 [768, 768], P(None, 'fsdp')
- grad_rel_table: float32 [12, 32], replicated
- grad_norm_ffn: float32 [768], P('fsdp')
- grad_weight_router: float32 [768, 4], P('fsdp')
- grad_expert_up: float32 [4, 768, 3072], P(None, 'fsdp', ('ctx', 'tp'))
- grad_expert_down: float32 [4, 3072, 768], P(None, ('ctx', 'tp'), 'fsdp')
Inputs may be any that keep to these rules, and one draw needn't show every extreme that they name: `seg_ids`: each group's 512 positions fall into at most 3 sequences whose numbers never fall along the positions; the longest has exactly 384 positions. `routes`: each token names two different experts. In each aligned block of 128 rows (the rows of one device) no expert is named more than 80 times, and in every draw some expert is named exactly 80 times in some block.
All inputs are finite; a program needn't handle non-finite values.
Results may differ from a plain program's by a relative error of at most 0.012.
Values may be sent and summed in bfloat16 or wider, within the bound.
A program may use at most 192 MiB of HBM per device.

v0:
```python
import jax
import jax.numpy as jnp
import numpy as np
from jax import lax
from jax.sharding import PartitionSpec as P

BUCKETS = 32
MAX_DISTANCE = 128
EPSILON = 1e-06
MASK_FILL = -1e30
F32 = jnp.float32
BF16 = jnp.bfloat16


def bucket_bounds(buckets, far_reach):
    exact_count = buckets // 2
    bounds = []
    for number in range(1, buckets):
        if number <= exact_count:
            bounds.append(number)
        else:
            exponent = (number - exact_count) / (buckets - exact_count)
            bounds.append(int(np.ceil(exact_count * (far_reach / exact_count) ** exponent)))
    return bounds


BOUNDS = bucket_bounds(BUCKETS, MAX_DISTANCE)


def rms_scale(values):
    return lax.rsqrt(jnp.mean(values * values, axis=-1, keepdims=True) + EPSILON)


def dot(a, b, ca, cb):
    return lax.dot_general(a, b, (((ca,), (cb,)), ((), ())), preferred_element_type=F32)


def exchange_sum(part, axis, dim):
    count = lax.axis_size(axis)
    size = part.shape[dim] // count
    me = lax.axis_index(axis)
    total = lax.dynamic_slice_in_dim(part, me * size, size, dim)
    for step in range(1, count):
        target = lax.rem(me + step, count)
        piece = lax.dynamic_slice_in_dim(part, target * size, size, dim).astype(BF16)
        total = total + lax.ppermute(
            piece, axis, [(i, (i + step) % count) for i in range(count)]
        ).astype(F32)
    return total


def local(
    tokens,
    seg_ids,
    routes,
    norm_attn,
    weight_qkv,
    weight_proj,
    rel_table,
    norm_ffn,
    weight_router,
    expert_up,
    expert_down,
    cotangent,
):
    rows = tokens.shape[1]
    width = tokens.shape[2]
    heads = rel_table.shape[0]
    head_size = width // heads
    ctx_count = lax.axis_size("ctx")
    heads_here = heads // ctx_count
    hw = heads_here * head_size
    experts = expert_up.shape[0]
    units = expert_up.shape[2]
    length = seg_ids.shape[1]
    score_scale = head_size ** (-0.5)
    ctx_index = lax.axis_index("ctx")
    fsdp_index = lax.axis_index("fsdp")
    own_width = norm_attn.shape[0]
    world = ("ctx", "tp")
    token_group = lax.all_gather(tokens[0], "ctx", axis=0, tiled=True)
    small = jnp.concatenate([norm_attn[None], norm_ffn[None], weight_router.T], axis=0)
    small = lax.all_gather(small, "fsdp", axis=1, tiled=True)
    gain_one = small[0].astype(F32)
    gain_two = small[1].astype(F32)
    router_t = small[2:]
    qkv_part = jnp.concatenate(
        [lax.dynamic_slice_in_dim(weight_qkv, s * width + ctx_index * hw, hw, 1) for s in range(3)],
        axis=1,
    )
    qkv_here = lax.all_gather(qkv_part, "fsdp", axis=0, tiled=True)
    proj_full = lax.all_gather(weight_proj, "fsdp", axis=1, tiled=True)
    route_all = lax.all_gather(routes[0], world, axis=0, tiled=True)
    up_t = lax.all_gather(
        jnp.swapaxes(expert_up, 1, 2).reshape(experts * units, own_width),
        "fsdp",
        axis=1,
        tiled=True,
    )
    down = lax.all_gather(
        expert_down.reshape(experts * units, own_width), "fsdp", axis=1, tiled=True
    )
    grad_all = lax.all_gather(cotangent[0], world, axis=0, tiled=True)
    block = MAX_DISTANCE
    table_here = lax.dynamic_slice_in_dim(rel_table, ctx_index * heads_here, heads_here, 0)
    offset = lax.broadcasted_iota(jnp.int32, (1, block, block), 1) - lax.broadcasted_iota(
        jnp.int32, (1, block, block), 2
    )

    def bias_block(distance):
        value = jnp.broadcast_to(table_here[:, 0][:, None, None], (heads_here, block, block))
        for number, bound in enumerate(BOUNDS, 1):
            value = jnp.where(distance >= bound, table_here[:, number][:, None, None], value)
        return value

    near = bias_block(offset)
    next_near = bias_block(offset + block)
    far = jnp.broadcast_to(table_here[:, BUCKETS - 1][:, None, None], (heads_here, block, block))
    blocks = length // block
    picks = {0: near, 1: next_near}
    bias = jnp.concatenate(
        [
            jnp.concatenate([picks.get(i - j, far) for j in range(blocks)], axis=2)
            for i in range(blocks)
        ],
        axis=1,
    )
    positions = jnp.arange(length, dtype=jnp.int32)
    segment = seg_ids[0]
    allowed = (segment[:, None] == segment[None, :]) & (positions[:, None] >= positions[None, :])
    bias = jnp.where(allowed[None], bias, MASK_FILL)
    inputs_group = token_group.astype(F32)
    normed_group = (inputs_group * rms_scale(inputs_group) * gain_one).astype(BF16)
    projected = dot(normed_group, qkv_here, 1, 0).astype(BF16)
    by_head = projected.reshape(length, 3, heads_here, head_size)
    query, key, value = (by_head[:, 0], by_head[:, 1], by_head[:, 2])
    scores = jnp.einsum("qhd,khd->hqk", query, key, preferred_element_type=F32) * score_scale + bias
    peak = jnp.max(scores, axis=-1, keepdims=True)
    weights = jnp.exp(scores - peak)
    probs = weights / jnp.sum(weights, axis=-1, keepdims=True)
    low_probs = probs.astype(BF16)
    attended = (
        jnp.einsum("hqk,khd->qhd", low_probs, value, preferred_element_type=F32)
        .astype(BF16)
        .reshape(length, hw)
    )
    mixed = lax.all_to_all(attended, "ctx", split_axis=0, concat_axis=1, tiled=True)
    inputs = tokens[0].astype(F32)
    scale_one = rms_scale(inputs)
    middle = inputs + dot(mixed, proj_full, 1, 0)
    scale_two = rms_scale(middle)
    normed_two = (middle * scale_two * gain_two).astype(BF16)
    normed_all = lax.all_gather(normed_two, world, axis=0, tiled=True)

    def gates_of(normed, route):
        logits = dot(normed, router_t, 1, 1)
        number = lax.broadcasted_iota(jnp.int32, (1, experts), 1)
        chosen = (route[:, 0:1] == number) | (route[:, 1:2] == number)
        masked = jnp.where(chosen, logits, MASK_FILL)
        raw = jnp.where(chosen, jnp.exp(masked - jnp.max(masked, axis=1, keepdims=True)), 0.0)
        return raw / jnp.sum(raw, axis=1, keepdims=True)

    gates_all = gates_of(normed_all, route_all)
    column = lax.broadcasted_iota(jnp.int32, (1, experts * units), 1) // units
    spread = gates_all[:, 0:1]
    for e in range(1, experts):
        spread = jnp.where(column >= e, gates_all[:, e : e + 1], spread)
    pre = dot(normed_all, up_t, 1, 1)
    reach = dot(grad_all, down, 1, 1)
    act, gelu_back = jax.vjp(jax.nn.gelu, pre)
    act = act.astype(BF16).astype(F32)
    gated = (act * spread).astype(BF16)
    product = act * reach
    dots_all = jnp.stack(
        [jnp.sum(jnp.where(column == e, product, 0.0), axis=1) for e in range(experts)], axis=0
    )
    grad_pre = gelu_back(reach * spread)[0].astype(BF16)
    total_rows = normed_all.shape[0]
    devices = total_rows // rows
    dots_all = jnp.swapaxes(dots_all.reshape(experts, devices, rows), 0, 1)
    dots_own = lax.psum_scatter(
        dots_all.reshape(devices, experts * rows), world, scatter_dimension=0, tiled=True
    )
    gate_dots = dots_own.reshape(experts, rows).T
    grad_normed_two = lax.psum_scatter(
        dot(grad_pre, up_t, 1, 0).astype(BF16), world, scatter_dimension=0, tiled=True
    ).astype(F32)
    result = lax.psum_scatter(
        dot(gated, down, 1, 0).astype(BF16), world, scatter_dimension=0, tiled=True
    ).astype(F32)
    output = (middle + result).astype(BF16)[None]
    grad_up = exchange_sum(dot(grad_pre, normed_all, 0, 0), "fsdp", 1)
    grad_up = jnp.swapaxes(grad_up.reshape(experts, units, own_width), 1, 2)
    grad_down = exchange_sum(dot(gated, grad_all, 0, 0), "fsdp", 1)
    grad_down = grad_down.reshape(experts, units, own_width)
    grad_out = cotangent[0].astype(F32)
    gates = gates_of(normed_two, routes[0])
    grad_logits = gates * (gate_dots - jnp.sum(gates * gate_dots, axis=1, keepdims=True))
    grad_normed_two = grad_normed_two + jnp.dot(
        grad_logits, router_t.astype(F32), precision=lax.Precision.HIGHEST
    )
    grad_router = lax.dot_general(
        grad_logits,
        normed_two.astype(F32),
        (((0,), (0,)), ((), ())),
        precision=lax.Precision.HIGHEST,
    )
    weighted_two = grad_normed_two * gain_two
    grad_gain_two = jnp.sum(grad_normed_two * middle * scale_two, axis=0)
    grad_middle = (
        grad_out
        + scale_two * weighted_two
        - middle * scale_two**3 * jnp.mean(weighted_two * middle, axis=1, keepdims=True)
    )
    grad_mid_group = lax.all_gather(grad_middle.astype(BF16), "ctx", axis=0, tiled=True)
    proj_rows = lax.dynamic_slice_in_dim(proj_full, ctx_index * hw, hw, 0)
    grad_attended = dot(grad_mid_group, proj_rows, 1, 1).astype(BF16)
    grad_heads = grad_attended.reshape(length, heads_here, head_size)
    grad_value = jnp.einsum("hqk,qhd->khd", low_probs, grad_heads, preferred_element_type=F32)
    grad_probs = jnp.einsum("qhd,khd->hqk", grad_heads, value, preferred_element_type=F32)
    grad_scores = (
        probs * (grad_probs - jnp.sum(probs * grad_probs, axis=-1, keepdims=True))
    ).astype(BF16)
    grad_query = (
        jnp.einsum("hqk,khd->qhd", grad_scores, key, preferred_element_type=F32) * score_scale
    )
    grad_key = (
        jnp.einsum("hqk,qhd->khd", grad_scores, query, preferred_element_type=F32) * score_scale
    )
    grad_qkv = jnp.concatenate(
        [
            grad_query.astype(BF16).reshape(length, hw),
            grad_key.astype(BF16).reshape(length, hw),
            grad_value.astype(BF16).reshape(length, hw),
        ],
        axis=1,
    )
    grad_normed_one = exchange_sum(dot(grad_qkv, qkv_here, 1, 1), "ctx", 0)
    weight_part = jnp.concatenate(
        [dot(normed_group, grad_qkv, 0, 0), dot(grad_mid_group, attended, 0, 0)], axis=1
    )
    weight_own = lax.psum_scatter(
        weight_part.astype(BF16), ("fsdp", "tp"), scatter_dimension=0, tiled=True
    )
    weight_all = lax.all_gather(weight_own, world, axis=0, tiled=True).astype(F32)
    weight_all = weight_all.reshape(ctx_count, own_width, 4 * hw)
    grad_weight_qkv = jnp.concatenate(
        [weight_all[c, :, s * hw : (s + 1) * hw] for s in range(3) for c in range(ctx_count)],
        axis=1,
    )
    grad_weight_proj = jnp.swapaxes(weight_all[:, :, 3 * hw :], 1, 2).reshape(width, own_width)

    def score_block(i, j):
        return grad_scores[:, i * block : (i + 1) * block, j * block : (j + 1) * block].astype(F32)

    near_sum = sum((score_block(i, i) for i in range(blocks)))
    next_sum = sum((score_block(i + 1, i) for i in range(blocks - 1)))
    far_sum = sum(
        (jnp.sum(score_block(i, j), axis=(1, 2)) for i in range(blocks) for j in range(i - 1))
    )
    lows = [0] + BOUNDS
    highs = BOUNDS + [2 * block]
    bucket_sums = [
        jnp.sum(jnp.where((offset >= lo) & (offset < hi), near_sum, 0.0), axis=(1, 2))
        + jnp.sum(
            jnp.where((offset + block >= lo) & (offset + block < hi), next_sum, 0.0), axis=(1, 2)
        )
        for lo, hi in zip(lows, highs)
    ]
    bucket_sums[-1] = bucket_sums[-1] + far_sum
    table_here_grad = jnp.stack(bucket_sums, axis=1)
    table_term = lax.dynamic_update_slice_in_dim(
        jnp.zeros((heads, BUCKETS), F32), table_here_grad, ctx_index * heads_here, 0
    )
    weighted_one = grad_normed_one * gain_one
    grad_gain_one = jnp.sum(grad_normed_one * inputs * scale_one, axis=0)
    grad_tokens = (
        grad_middle
        + scale_one * weighted_one
        - inputs * scale_one**3 * jnp.mean(weighted_one * inputs, axis=1, keepdims=True)
    )
    packed = jnp.concatenate(
        [grad_gain_one, grad_gain_two, grad_router.reshape(-1), table_term.reshape(-1)]
    ).reshape(-1, 128)
    packed = lax.psum(packed, ("fsdp", "ctx", "tp")).reshape(-1)
    gains = packed[: (2 + experts) * width].reshape(2 + experts, width)
    gains = lax.dynamic_slice_in_dim(gains, fsdp_index * own_width, own_width, 1)
    table_grad = packed[(2 + experts) * width :].reshape(heads, BUCKETS)
    return (
        output,
        grad_tokens[None],
        gains[0],
        grad_weight_qkv,
        grad_weight_proj,
        table_grad,
        gains[1],
        gains[2:].T,
        grad_up,
        grad_down,
    )


def solution(mesh):
    rows = P(("fsdp", "tp"), "ctx", None)
    in_specs = (
        rows,
        P(("fsdp", "tp"), None),
        rows,
        P("fsdp"),
        P("fsdp", None),
        P(None, "fsdp"),
        P(),
        P("fsdp"),
        P("fsdp", None),
        P(None, "fsdp", ("ctx", "tp")),
        P(None, ("ctx", "tp"), "fsdp"),
        rows,
    )
    out_specs = (
        rows,
        rows,
        P("fsdp"),
        P("fsdp", None),
        P(None, "fsdp"),
        P(),
        P("fsdp"),
        P("fsdp", None),
        P(None, "fsdp", ("ctx", "tp")),
        P(None, ("ctx", "tp"), "fsdp"),
    )
    return jax.shard_map(local, mesh=mesh, in_specs=in_specs, out_specs=out_specs, check_vma=False)
```

profile of v0, /device:TPU:0, one launch (start us, length us, event | category | flops | bytes accessed | tf_op | source)
XLA Modules:
  0.0 534.5 jit_solution(10073200459211450725)
XLA Ops:
  9.8 1.4 constant_dynamic-slice_fusion.4
  11.4 20.5 %all_gather.35 = bf16[768,576]{1,0:T(8,128)(2,1)S(1)} all-gather(bf16[384,576]{1,0:T(8,128)(2,1)S(1)} %pad_maximum_fusion.2), channel_id=1, replica_groups=mesh['fsdp'=2,'ctx'=4,'tp'=4] {'fsdp'}, dimensions={0}, use_global_device_ids=true | all-gather | bytes 1327104 | tf_op jit(solution)/shard_map/all_gather | solution.py:91
  32.0 4.9 all_gather.34
  37.6 8.4 %all-gather = bf16[1,512,768]{2,1,0:T(8,128)(2,1)S(1)} all-gather(bf16[1,128,768]{2,1,0:T(8,128)(2,1)S(1)} %copy-done.6), channel_id=2, replica_groups=mesh['fsdp'=2,'ctx'=4,'tp'=4] {'ctx'}, dimensions={1}, use_global_device_ids=true | all-gather | bytes 983040 | tf_op jit(solution)/shard_map/all_gather | solution.py:81
  49.7 1.9 fusion.256
  51.6 4.9 convolution_convert_fusion.6
  56.7 8.4 %all_to_all.19 = bf16[4,128,192]{1,2,0:T(8,128)(2,1)} all-to-all(bf16[4,128,192]{1,2,0:T(8,128)(2,1)S(1)} %copy.59), channel_id=1, replica_groups=mesh['fsdp'=2,'ctx'=4,'tp'=4] {'ctx'}, dimensions={0} | all-to-all | bytes 393216 | tf_op jit(solution)/shard_map/all_to_all | solution.py:147
  65.0 1.8 multiply_reduce_fusion.3
  70.2 31.9 %all-gather.1 = s32[1,2048,2]{1,2,0:T(2,128)S(1)} all-gather(s32[1,128,2]{1,2,0:T(2,128)S(1)} %copy-done.68), channel_id=3, replica_groups=mesh['fsdp'=2,'ctx'=4,'tp'=4] {'ctx','tp'}, dimensions={1}, use_global_device_ids=true | all-gather | bytes 17408 | tf_op jit(solution)/shard_map/all_gather | solution.py:93
  104.5 10.3 %all-gather.12.cloned.1.call-done = bf16[2048,768]{1,0:T(8,128)(2,1)} async-done(((bf16[128,768]{1,0:T(8,128)(2,1)}), bf16[2048,768]{1,0:T(8,128)(2,1)}) %all-gather.12.cloned.1.call-update) | async-done | bytes 3145744 | tf_op jit(solution)/shard_map/all_gather | solution.py:153
  114.9 2.8 fusion.257
  118.4 19.6 %all-gather.14.cloned.1.call-done = bf16[768,768]{1,0:T(8,128)(2,1)} async-done(((bf16[768,384]{1,0:T(8,128)(2,1)}), bf16[768,768]{1,0:T(8,128)(2,1)}) %all-gather.14.cloned.1.call-update) | async-done | bytes 1179664 | tf_op jit(solution)/shard_map/all_gather | solution.py:94
  138.0 7.5 %fusion.259 = f32[2048,768]{0,1:T(8,128)} fusion(bf16[2048,768]{1,0:T(8,128)(2,1)} %all-gather.12.cloned.1.call-done, bf16[768,768]{1,0:T(8,128)(2,1)} %all-gather.14.cloned.1.call-done), kind=kOutput, calls=%fused_computation.499 | convolution fusion | flops 2415919104 | bytes 10616832 | tf_op jit(solution)/shard_map/dot_general | solution.py:35
  145.5 16.7 %all-gather.16.cloned.1.call-done = bf16[768,768]{1,0:T(8,128)(2,1)} async-done(((bf16[768,384]{1,0:T(8,128)(2,1)}), bf16[768,768]{1,0:T(8,128)(2,1)}) %all-gather.16.cloned.1.call-update) | async-done | bytes 1179664 | tf_op jit(solution)/shard_map/all_gather | solution.py:100
  162.2 47.4 %all-gather.20.cloned.1.call-done = bf16[1,2048,768]{2,1,0:T(8,128)(2,1)} async-done(((bf16[1,128,768]{2,1,0:T(8,128)(2,1)}), bf16[1,2048,768]{2,1,0:T(8,128)(2,1)}) %all-gather.20.cloned.1.call-update) | async-done | bytes 3145744 | tf_op jit(solution)/shard_map/all_gather | solution.py:103
  209.6 15.3 %select_reduce_fusion.3 = (f32[2048]{0:T(1024)}, f32[2048]{0:T(1024)}, f32[2048]{0:T(1024)}, f32[2048]{0:T(1024)}, bf16[2048,768]{0,1:T(8,128)(2,1)}, /*index=5*/bf16[2048,768]{0,1:T(8,128)(2,1)S(1)}) fusion(pred[768]{0:T(1024)(128)(4,1)} %get-tuple-element.174, pred[768]{0:T(1024)(128)(4,1)} %get-tuple-element.175, pred[768]{0:T(1024)(128)(4,1)} %get-tuple-element.170, ...), kind=kOutput, calls=%fused_computation.16 | convolution fusion | flops 2472534016 | bytes 16979200 | tf_op jit(solution)/shard_map/dot_general | solution.py:35
  224.9 1.7 copy-done.77
  226.6 4.1 convolution_convert_fusion
  249.5 7.5 %convolution_convert_fusion.1 = bf16[2048,768]{1,0:T(8,128)(2,1)} fusion(bf16[768,768]{1,0:T(8,128)(2,1)} %all-gather.16.cloned.1.call-done, bf16[2048,768]{0,1:T(8,128)(2,1)} %get-tuple-element.126, f32[2048]{0:T(1024)S(1)} %bitcast.258, f32[2048]{0:T(1024)} %bitcast.261, f32[2048]{0:T(1024)} %bitcast.264, f32[2048]{0:T(1024)S(1)} %bitcast.255, ...), kind=kOutput, calls=%fused_computation.20 | convolution fusion | flops 2426929152 | bytes 7506176 | tf_op jit(solution)/shard_map/dot_general | solution.py:35
  263.2 6.3 %fusion.10 = f32[768,768]{1,0:T(8,128)S(1)} fusion(bf16[1,2048,768]{2,1,0:T(8,128)(2,1)} %all-gather.20.cloned.1.call-done, bf16[2048,768]{0,1:T(8,128)(2,1)} %get-tuple-element.126, f32[2048]{0:T(1024)} %bitcast.259, f32[2048]{0:T(1024)} %bitcast.262, f32[2048]{0:T(1024)} %bitcast.265, f32[2048]{0:T(1024)} %bitcast.256, ...), kind=kOutput, calls=%fused_computation.23 | convolution fusion | flops 2425356288 | bytes 8685824 | tf_op jit(solution)/shard_map/dot_general | solution.py:35
  270.5 1.5 collective-permute-start.4
  272.0 2.6 fusion.260
  277.5 60.8 %all-reduce = f32[16,512]{1,0:T(8,128)} all-reduce(f32[16,512]{1,0:T(8,128)} %bitcast.247), channel_id=7, replica_groups=mesh['fsdp'=2,'ctx'=4,'tp'=4] {'ctx','tp'}, use_global_device_ids=true, to_apply=%region_14.15.clone | all-reduce | flops 8192 | bytes 65536
  340.9 1.7 fusion.245
  343.9 2.7 convert_add_fusion
  346.7 2.2 convert_add_fusion.1
  348.9 2.8 multiply_reduce_fusion.1
  351.7 13.4 %reduce-scatter.6.cloned.1.call-done = bf16[128,768]{1,0:T(8,128)(2,1)} async-done(((bf16[2048,768]{1,0:T(8,128)(2,1)}), bf16[128,768]{1,0:T(8,128)(2,1)}) %reduce-scatter.6.cloned.1.call-update) | async-done | bytes 196624 | tf_op jit(solution)/shard_map/reduce_scatter | solution.py:188
  365.1 2.3 fusion.252
  367.3 8.1 %all_gather.42 = bf16[512,768]{1,0:T(8,128)(2,1)S(1)} all-gather(bf16[128,768]{1,0:T(8,128)(2,1)S(1)} %get-tuple-element.124), channel_id=1, replica_groups=mesh['fsdp'=2,'ctx'=4,'tp'=4] {'ctx'}, dimensions={0}, use_global_device_ids=true | all-gather | bytes 983040 | tf_op jit(solution)/shard_map/all_gather | solution.py:215
  379.1 2.7 multiply_convert_fusion.1
  384.2 4.5 convolution_convert_fusion.5
  389.2 1.9 convolution_convert_fusion.2
  391.4 1.5 copy.101
  393.3 2.1 select_reduce_fusion.4
  395.5 2.1 select_reduce_fusion.5
  412.1 1.4 select_reduce_fusion.41
  413.5 42.9 %reduce-scatter.10.cloned.1.call-done = bf16[96,768]{1,0:T(8,128)(2,1)} async-done(((bf16[768,768]{1,0:T(8,128)(2,1)}), bf16[96,768]{1,0:T(8,128)(2,1)}) %reduce-scatter.10.cloned.1.call-update) | async-done | bytes 147472 | tf_op jit(solution)/shard_map/reduce_scatter | solution.py:242
  457.8 1.8 fusion.31
  460.9 1.5 collective-permute-start.1
  464.2 3.2 collective-permute-done
  467.5 1.5 collective-permute-done.1
  469.0 3.9 collective-permute-done.2
  474.1 40.1 %psum.7 = f32[39,128]{1,0:T(8,128)S(1)} all-reduce(f32[39,128]{1,0:T(8,128)S(1)} %maximum_bitcast_fusion), channel_id=1, replica_groups=mesh['fsdp'=2,'ctx'=4,'tp'=4] {'fsdp','ctx','tp'}, use_global_device_ids=true, to_apply=%region_89.90 | all-reduce | flops 4992 | bytes 39936 | tf_op jit(solution)/shard_map/psum | solution.py:285
  517.2 2.1 convert.13
  519.2 1.9 slice_bitcast_fusion.1
  521.7 1.5 copy.96
  523.1 4.7 concatenate.45
  (376 shorter events, 76.3 us)
Async XLA Ops:
  7.2 24.8 %copy-start.73 = (bf16[384]{0:T(512)(128)(2,1)S(1)}, bf16[384]{0:T(512)(128)(2,1)}, u32[]{:S(2)}) copy-start(bf16[384]{0:T(512)(128)(2,1)} %param.15) | copy-start | bytes 2308
  7.2 24.8 %copy-start.74 = (bf16[384]{0:T(512)(128)(2,1)S(1)}, bf16[384]{0:T(512)(128)(2,1)}, u32[]{:S(2)}) copy-start(bf16[384]{0:T(512)(128)(2,1)} %param.19) | copy-start | bytes 2308
  7.2 24.8 %copy-start.70 = (bf16[384,4]{0,1:T(4,128)(2,1)S(1)}, bf16[384,4]{0,1:T(4,128)(2,1)}, u32[]{:S(2)}) copy-start(bf16[384,4]{0,1:T(4,128)(2,1)} %param.20) | copy-start | bytes 9220
  7.2 30.3 %copy-start.6 = (bf16[1,128,768]{2,1,0:T(8,128)(2,1)S(1)}, bf16[1,128,768]{2,1,0:T(8,128)(2,1)}, u32[]{:S(2)}) copy-start(bf16[1,128,768]{2,1,0:T(8,128)(2,1)} %param.12) | copy-start | bytes 589828
  7.2 57.8 %all-gather.10.cloned.1.call-start = ((), (), s32[]{:S(2)}) async-start(), calls=%async_computation.4 | async-start | bytes 1769472 | tf_op jit(solution)/shard_map/all_gather | solution.py:92
  8.0 106.9 %all-gather.12.cloned.1.call-start = ((), (), s32[]{:S(2)}) async-start(), calls=%async_computation.5 | async-start | bytes 3342336 | tf_op jit(solution)/shard_map/all_gather | solution.py:153
  9.2 37.1 %copy-start.59 = (s32[1,512]{1,0:T(1,128)S(1)}, s32[1,512]{1,0:T(1,128)}, u32[]{:S(2)}) copy-start(s32[1,512]{1,0:T(1,128)} %param.13) | copy-start | bytes 6148
  32.0 16.8 %copy-start.15 = (bf16[768,576]{1,0:T(8,128)(2,1)}, bf16[768,576]{1,0:T(8,128)(2,1)S(1)}, u32[]{:S(2)}) copy-start(bf16[768,576]{1,0:T(8,128)(2,1)S(1)} %all_gather.35) | copy-start | bytes 2654212
  37.6 11.2 %copy-start.52 = (f32[768]{0:T(1024)}, f32[768]{0:T(1024)S(1)}, u32[]{:S(2)}) copy-start(f32[768]{0:T(1024)S(1)} %get-tuple-element.88) | copy-start | bytes 9220
  37.6 29.9 %copy-start.25 = (f32[768]{0:T(1024)}, f32[768]{0:T(1024)S(1)}, u32[]{:S(2)}) copy-start(f32[768]{0:T(1024)S(1)} %get-tuple-element.87) | copy-start | bytes 9220
  51.6 326.1 %copy-start.2 = (f32[3,512,512]{1,2,0:T(8,128)}, f32[3,512,512]{1,2,0:T(8,128)S(1)}, u32[]{:S(2)}) copy-start(f32[3,512,512]{1,2,0:T(8,128)S(1)} %get-tuple-element.160) | copy-start | bytes 9437188
  56.5 8.5 %copy-start.17 = (bf16[3,64,512]{2,1,0:T(8,128)(2,1)}, bf16[3,64,512]{2,1,0:T(8,128)(2,1)S(1)}, u32[]{:S(2)}) copy-start(bf16[3,64,512]{2,1,0:T(8,128)(2,1)S(1)} %convolution_convert_fusion.6) | copy-start | bytes 589828
  56.5 13.6 %copy-start.68 = (s32[1,128,2]{1,2,0:T(2,128)S(1)}, s32[1,128,2]{1,2,0:T(2,128)}, u32[]{:S(2)}) copy-start(s32[1,128,2]{1,2,0:T(2,128)} %param.14) | copy-start | bytes 3076
  67.4 37.1 %copy-start.67 = (f32[128]{0:T(128)}, f32[128]{0:T(128)S(1)}, u32[]{:S(2)}) copy-start(f32[128]{0:T(128)S(1)} %get-tuple-element.158) | copy-start | bytes 1540
  68.2 69.8 %all-gather.14.cloned.1.call-start = ((), (), s32[]{:S(2)}) async-start(), calls=%async_computation.6 | async-start | bytes 1769472 | tf_op jit(solution)/shard_map/all_gather | solution.py:94
  69.0 93.3 %all-gather.16.cloned.1.call-start = ((), (), s32[]{:S(2)}) async-start(), calls=%async_computation.7 | async-start | bytes 1769472 | tf_op jit(solution)/shard_map/all_gather | solution.py:100
  69.6 140.1 %all-gather.20.cloned.1.call-start = ((), (), s32[]{:S(2)}) async-start(), calls=%async_computation.11 | async-start | bytes 3342336 | tf_op jit(solution)/shard_map/all_gather | solution.py:103
  70.1 278.7 %reduce-scatter.8.cloned.1.call-start = ((), (), s32[]{:S(2)}) async-start(), calls=%async_computation.9 | async-start | bytes 3342336 | tf_op jit(solution)/shard_map/reduce_scatter | solution.py:185
  118.4 131.1 %copy-start.60 = (f32[2048,1]{0,1:T(1,128)}, f32[2048,1]{0,1:T(1,128)S(1)}, u32[]{:S(2)}) copy-start(f32[2048,1]{0,1:T(1,128)S(1)} %get-tuple-element.147) | copy-start | bytes 24580
  118.4 131.1 %copy-start.61 = (f32[2048,1]{0,1:T(1,128)}, f32[2048,1]{0,1:T(1,128)S(1)}, u32[]{:S(2)}) copy-start(f32[2048,1]{0,1:T(1,128)S(1)} %get-tuple-element.148) | copy-start | bytes 24580
  209.6 17.0 %copy-start.76 = (bf16[768,768]{1,0:T(8,128)(2,1)S(1)}, bf16[768,768]{1,0:T(8,128)(2,1)}, u32[]{:S(2)}) copy-start(bf16[768,768]{1,0:T(8,128)(2,1)} %all-gather.14.cloned.1.call-done) | copy-start | bytes 3538948
  230.7 134.4 %reduce-scatter.6.cloned.1.call-start = ((), (), s32[]{:S(2)}) async-start(), calls=%async_computation.8 | async-start | bytes 3342336 | tf_op jit(solution)/shard_map/reduce_scatter | solution.py:188
  257.0 199.4 %reduce-scatter.10.cloned.1.call-start = ((), (), s32[]{:S(2)}) async-start(), calls=%async_computation.12 | async-start | bytes 1327104 | tf_op jit(solution)/shard_map/reduce_scatter | solution.py:242
  261.5 8.0 %copy-start.56 = (s32[128]{0:T(128)}, s32[128]{0:T(128)S(1)}, u32[]{:S(2)}) copy-start(s32[128]{0:T(128)S(1)} %get-tuple-element.154) | copy-start | bytes 1540
  262.6 6.9 %copy-start.58 = (f32[128]{0:T(128)}, f32[128]{0:T(128)S(1)}, u32[]{:S(2)}) copy-start(f32[128]{0:T(128)S(1)} %get-tuple-element.165) | copy-start | bytes 1540
  263.2 8.8 %copy-start.3 = (bf16[2048,768]{1,0:T(8,128)(2,1)S(1)}, bf16[2048,768]{1,0:T(8,128)(2,1)}, u32[]{:S(2)}) copy-start(bf16[2048,768]{1,0:T(8,128)(2,1)} %all-gather.12.cloned.1.call-done) | copy-start | bytes 9437188
  263.2 8.8 %copy-start.78 = (bf16[2048,768]{0,1:T(8,128)(2,1)S(1)}, bf16[2048,768]{0,1:T(8,128)(2,1)}, u32[]{:S(2)}) copy-start(bf16[2048,768]{0,1:T(8,128)(2,1)} %copy-done.77) | copy-start | bytes 9437188
  270.5 6.4 %copy-start.62 = (f32[2048]{0:T(1024)S(1)}, f32[2048]{0:T(1024)}, u32[]{:S(2)}) copy-start(f32[2048]{0:T(1024)} %get-tuple-element.10) | copy-start | bytes 24580
  270.5 6.4 %copy-start.63 = (f32[2048]{0:T(1024)S(1)}, f32[2048]{0:T(1024)}, u32[]{:S(2)}) copy-start(f32[2048]{0:T(1024)} %get-tuple-element.11) | copy-start | bytes 24580
  270.5 6.4 %copy-start.64 = (f32[2048]{0:T(1024)S(1)}, f32[2048]{0:T(1024)}, u32[]{:S(2)}) copy-start(f32[2048]{0:T(1024)} %get-tuple-element.12) | copy-start | bytes 24580
  270.5 6.4 %copy-start.65 = (f32[2048]{0:T(1024)S(1)}, f32[2048]{0:T(1024)}, u32[]{:S(2)}) copy-start(f32[2048]{0:T(1024)} %get-tuple-element.13) | copy-start | bytes 24580
  270.5 73.4 %collective-permute-start.4 = (bf16[768,384]{1,0:T(8,128)(2,1)}, bf16[768,384]{1,0:T(8,128)(2,1)}, u32[]{:S(2)}, u32[]{:S(2)}) collective-permute-start(bf16[768,384]{1,0:T(8,128)(2,1)} %dynamic-slice_convert_fusion), channel_id=1, source_target_pairs={{0,16},{16,0},{1,17},{17,1},{2,18},{18,2},{3,19},{19,3},{4,20},{20... | collective-permute-start | bytes 1769480 | tf_op jit(solution)/shard_map/ppermute | solution.py:46
  276.3 70.4 %collective-permute-start.3 = (bf16[768,384]{1,0:T(8,128)(2,1)}, bf16[768,384]{1,0:T(8,128)(2,1)}, u32[]{:S(2)}, u32[]{:S(2)}) collective-permute-start(bf16[768,384]{1,0:T(8,128)(2,1)} %dynamic-slice_convert_fusion.1), channel_id=1, source_target_pairs={{0,16},{16,0},{1,17},{17,1},{2,18},{18,2},{3,19},{19,3},{4,20},{20... | collective-permute-start | bytes 1769480 | tf_op jit(solution)/shard_map/ppermute | solution.py:46
  276.9 72.0 %copy-start.26 = (f32[768]{0:T(1024)S(1)}, f32[768]{0:T(1024)}, u32[]{:S(2)}) copy-start(f32[768]{0:T(1024)} %copy-done.25) | copy-start | bytes 9220
  365.1 12.6 %copy-start.21 = (bf16[512,576]{0,1:T(8,128)(2,1)S(1)}, bf16[512,576]{0,1:T(8,128)(2,1)}, u32[]{:S(2)}) copy-start(bf16[512,576]{0,1:T(8,128)(2,1)} %copy-done.20) | copy-start | bytes 1769476
  391.4 66.3 %copy-start.23 = (bf16[3,64,512]{2,1,0:T(8,128)(2,1)S(1)}, bf16[3,64,512]{2,1,0:T(8,128)(2,1)}, u32[]{:S(2)}) copy-start(bf16[3,64,512]{2,1,0:T(8,128)(2,1)} %fusion.17) | copy-start | bytes 589828
  391.4 66.3 %copy-start.24 = (bf16[3,64,512]{2,1,0:T(8,128)(2,1)S(1)}, bf16[3,64,512]{2,1,0:T(8,128)(2,1)}, u32[]{:S(2)}) copy-start(bf16[3,64,512]{2,1,0:T(8,128)(2,1)} %fusion.18) | copy-start | bytes 589828
  392.9 64.9 %copy-start.16 = (bf16[768,576]{1,0:T(8,128)(2,1)S(1)}, bf16[768,576]{1,0:T(8,128)(2,1)}, u32[]{:S(2)}) copy-start(bf16[768,576]{1,0:T(8,128)(2,1)} %copy-done.15) | copy-start | bytes 2654212
  392.9 124.3 %all-gather.18.cloned.1.call-start = ((), (), s32[]{:S(2)}) async-start(), calls=%async_computation.10 | async-start | bytes 2506752 | tf_op jit(solution)/shard_map/all_gather | solution.py:245
  397.7 75.2 %copy-start.7 = (bf16[1,128,768]{2,1,0:T(8,128)(2,1)S(1)}, bf16[1,128,768]{2,1,0:T(8,128)(2,1)}, u32[]{:S(2)}) copy-start(bf16[1,128,768]{2,1,0:T(8,128)(2,1)} %param.12) | copy-start | bytes 589828
  397.7 75.2 %copy-start.71 = (f32[128]{0:T(128)S(1)}, f32[128]{0:T(128)}, u32[]{:S(2)}) copy-start(f32[128]{0:T(128)} %get-tuple-element.156) | copy-start | bytes 1540
  457.8 16.3 %copy-start.51 = (f32[3072]{0:T(1024)S(1)}, f32[3072]{0:T(1024)}, u32[]{:S(2)}) copy-start(f32[3072]{0:T(1024)} %reshape.1329) | copy-start | bytes 36868
  457.8 16.3 %copy-start.57 = (f32[768]{0:T(1024)S(1)}, f32[768]{0:T(1024)}, u32[]{:S(2)}) copy-start(f32[768]{0:T(1024)} %get-tuple-element.17) | copy-start | bytes 9220
  457.8 58.5 %copy-start.11 = (f32[128,768]{1,0:T(8,128)S(1)}, f32[128,768]{1,0:T(8,128)}, u32[]{:S(2)}) copy-start(f32[128,768]{1,0:T(8,128)} %get-tuple-element.125) | copy-start | bytes 1179652
  457.8 58.5 %copy-start.75 = (f32[128]{0:T(128)S(1)}, f32[128]{0:T(128)}, u32[]{:S(2)}) copy-start(f32[128]{0:T(128)} %get-tuple-element.155) | copy-start | bytes 1540
  460.8 6.6 %collective-permute-start = (bf16[128,768]{1,0:T(8,128)(2,1)S(1)}, bf16[128,768]{1,0:T(8,128)(2,1)S(1)}, u32[]{:S(2)}, u32[]{:S(2)}) collective-permute-start(bf16[128,768]{1,0:T(8,128)(2,1)S(1)} %get-tuple-element.143), channel_id=1, source_target_pairs={{0,4},{4,8},{8,12},{12,0},{1,5},{5,9},{9,13},{13,1},{2,6},{6,10},{... | collective-permute-start | bytes 589832 | tf_op jit(solution)/shard_map/ppermute | solution.py:46
  460.9 8.1 %collective-permute-start.1 = (bf16[128,768]{1,0:T(8,128)(2,1)S(1)}, bf16[128,768]{1,0:T(8,128)(2,1)S(1)}, u32[]{:S(2)}, u32[]{:S(2)}) collective-permute-start(bf16[128,768]{1,0:T(8,128)(2,1)S(1)} %get-tuple-element.145), channel_id=1, source_target_pairs={{0,8},{4,12},{8,0},{12,4},{1,9},{5,13},{9,1},{13,5},{2,10},{6,14},... | collective-permute-start | bytes 589832 | tf_op jit(solution)/shard_map/ppermute | solution.py:46
  462.4 10.4 %collective-permute-start.2 = (bf16[128,768]{1,0:T(8,128)(2,1)S(1)}, bf16[128,768]{1,0:T(8,128)(2,1)S(1)}, u32[]{:S(2)}, u32[]{:S(2)}) collective-permute-start(bf16[128,768]{1,0:T(8,128)(2,1)S(1)} %get-tuple-element.144), channel_id=1, source_target_pairs={{0,12},{4,0},{8,4},{12,8},{1,13},{5,1},{9,5},{13,9},{2,14},{6,2},{... | collective-permute-start | bytes 589832 | tf_op jit(solution)/shard_map/ppermute | solution.py:46
  (45 other events, 135.1 us)
Sparse Core Ops, SparseCore 0:
  9.6 29.6 all-gather.9
  68.4 46.4 all-gather.11
  116.4 21.5 all-gather.13
  139.4 22.7 all-gather.15
  164.4 45.1 all-gather.19
  230.8 65.1 reduce-scatter.7
  299.8 65.2 reduce-scatter.5
  393.0 63.3 reduce-scatter.9
  458.7 42.8 all-gather.17
where the time goes:
time: 542 us; the launch traced here: 535 us
  blocking collectives  183 us (34%)
  waiting for transfers between devices  161 us (30%)
  matrix products  73.5 us (14%)
  other arithmetic  64.2 us (12%)
  local copies, waits for them, and re-layouts  31 us (6%)
  between operations  15.5 us (3%)
  starting transfers between devices  5.8 us (1%)
    unnamed x1, blocking collectives  60.8 us
    dot_general x14, matrix products, dot(): lax.dot_general(a, b, (((ca,), (cb,)), ((), ())), preferred_element_type=...  55.1 us
    all_gather x1, waiting for transfers between devices, local(): grad_all = lax.all_gather(cotangent[0], world, axis=0, tiled=True)  47.4 us
    reduce_scatter x1, waiting for transfers between devices, local(): lax.psum_scatter(weight_part.astype(BF16), ('fsdp', 'tp'), scatter_dimens...  42.9 us
    psum x1, blocking collectives, local(): packed = lax.psum(packed, ('fsdp', 'ctx', 'tp')).reshape(-1)  40.1 us
    all_gather x1, blocking collectives, local(): route_all = lax.all_gather(routes[0], world, axis=0, tiled=True)  31.9 us
    all_gather x1, blocking collectives, local(): qkv_here = lax.all_gather(qkv_part, 'fsdp', axis=0, tiled=True)  20.5 us
    all_gather x1, waiting for transfers between devices, local(): lax.all_gather(jnp.swapaxes(expert_up, 1, 2).reshape(experts * units, own...  19.6 us
  transfers between devices with their start and end apart: 14, of which 9 were waited for; matrix products, arithmetic and copies ran while one was open for 21% of the time, Pallas kernels for 0%

commit v1 on v0

--- a/solution.py
+++ b/solution.py
@@ -10,6 +10,11 @@
 MASK_FILL = -1e30
 F32 = jnp.float32
 BF16 = jnp.bfloat16
+
+
+def add_all(array, mesh_axis):
+    blocks = lax.all_gather(array, mesh_axis)
+    return jnp.sum(blocks, axis=0)
 
 
 def bucket_bounds(buckets, far_reach):
@@ -282,7 +287,7 @@
     packed = jnp.concatenate(
         [grad_gain_one, grad_gain_two, grad_router.reshape(-1), table_term.reshape(-1)]
     ).reshape(-1, 128)
-    packed = lax.psum(packed, ("fsdp", "ctx", "tp")).reshape(-1)
+    packed = add_all(packed, ("fsdp", "ctx", "tp")).reshape(-1)
     gains = packed[: (2 + experts) * width].reshape(2 + experts, width)
     gains = lax.dynamic_slice_in_dim(gains, fsdp_index * own_width, own_width, 1)
     table_grad = packed[(2 + experts) * width :].reshape(heads, BUCKETS)

time: 542 us -> 577 us (1.065)
  blocking collectives: 183 us -> 217 us
  waiting for transfers between devices: 161 us -> 176 us
  other arithmetic: 64.2 us -> 50.9 us
    all_gather x0 -> x1, blocking collectives: none -> 74.3 us  [add_all(): blocks = lax.all_gather(array, mesh_axis)]
    psum x1 -> x0, blocking collectives: 40.1 us -> none  [local(): packed = lax.psum(packed, ('fsdp', 'ctx', 'tp')).reshape(-1)]
    reduce_scatter x1, waiting for transfers between devices: 42.9 us -> 57.7 us  [local(): lax.psum_scatter(weight_part.astype(BF16), ('fsdp', 'tp'), scatter_dimens...]
    add x31, other arithmetic: 11.4 us -> 0.12 us  [local(): jnp.sum(jnp.where((offset >= lo) & (offset < hi), near_sum, 0.0), axis=(1...]
  transfers between devices with their start and end apart: 14 -> 14, of which waited for: 9 -> 9; matrix products, arithmetic and copies ran while one was open for 21% -> 17% of each run, Pallas kernels for 0% -> 0%
where the time goes in v1:
time: 577 us; the launch traced here: 571 us
  blocking collectives  217 us (38%)
  waiting for transfers between devices  176 us (31%)
  matrix products  73.5 us (13%)
  other arithmetic  50.9 us (9%)
  local copies, waits for them, and re-layouts  31 us (5%)
  between operations  15.8 us (3%)
  starting transfers between devices  6.07 us (1%)
    all_gather x1, blocking collectives, add_all(): blocks = lax.all_gather(array, mesh_axis)  74.3 us
    unnamed x1, blocking collectives  60.6 us
    reduce_scatter x1, waiting for transfers between devices, local(): lax.psum_scatter(weight_part.astype(BF16), ('fsdp', 'tp'), scatter_dimens...  57.7 us
    dot_general x14, matrix products, dot(): lax.dot_general(a, b, (((ca,), (cb,)), ((), ())), preferred_element_type=...  55 us
    all_gather x1, waiting for transfers between devices, local(): grad_all = lax.all_gather(cotangent[0], world, axis=0, tiled=True)  47.4 us
    all_gather x1, blocking collectives, local(): route_all = lax.all_gather(routes[0], world, axis=0, tiled=True)  31.8 us
    all_gather x1, blocking collectives, local(): qkv_here = lax.all_gather(qkv_part, 'fsdp', axis=0, tiled=True)  20.5 us
    all_gather x1, waiting for transfers between devices, local(): lax.all_gather(jnp.swapaxes(expert_up, 1, 2).reshape(experts * units, own...  19.6 us
  transfers between devices with their start and end apart: 14, of which 9 were waited for; matrix products, arithmetic and copies ran while one was open for 17% of the time, Pallas kernels for 0%

profile of v1, /device:TPU:0, one launch (start us, length us, event | category | flops | bytes accessed | tf_op | source)
XLA Modules:
  0.0 570.5 jit_solution(11758089445244145037)
XLA Ops:
  9.8 1.4 constant_dynamic-slice_fusion.4
  11.4 20.5 %all_gather.38 = bf16[768,576]{1,0:T(8,128)(2,1)S(1)} all-gather(bf16[384,576]{1,0:T(8,128)(2,1)S(1)} %pad_maximum_fusion.2), channel_id=1, replica_groups=mesh['fsdp'=2,'ctx'=4,'tp'=4] {'fsdp'}, dimensions={0}, use_global_device_ids=true | all-gather | bytes 1327104 | tf_op jit(solution)/shard_map/all_gather | solution.py:96
  32.0 4.9 all_gather.37
  37.6 8.4 %all-gather = bf16[1,512,768]{2,1,0:T(8,128)(2,1)S(1)} all-gather(bf16[1,128,768]{2,1,0:T(8,128)(2,1)S(1)} %copy-done.6), channel_id=2, replica_groups=mesh['fsdp'=2,'ctx'=4,'tp'=4] {'ctx'}, dimensions={1}, use_global_device_ids=true | all-gather | bytes 983040 | tf_op jit(solution)/shard_map/all_gather | solution.py:86
  49.7 1.9 fusion.256
  51.6 4.9 convolution_convert_fusion.6
  56.7 8.4 %all_to_all.19 = bf16[4,128,192]{1,2,0:T(8,128)(2,1)} all-to-all(bf16[4,128,192]{1,2,0:T(8,128)(2,1)S(1)} %copy.59), channel_id=1, replica_groups=mesh['fsdp'=2,'ctx'=4,'tp'=4] {'ctx'}, dimensions={0} | all-to-all | bytes 393216 | tf_op jit(solution)/shard_map/all_to_all | solution.py:152
  65.0 1.8 multiply_reduce_fusion.3
  70.2 31.8 %all-gather.1 = s32[1,2048,2]{1,2,0:T(2,128)S(1)} all-gather(s32[1,128,2]{1,2,0:T(2,128)S(1)} %copy-done.80), channel_id=3, replica_groups=mesh['fsdp'=2,'ctx'=4,'tp'=4] {'ctx','tp'}, dimensions={1}, use_global_device_ids=true | all-gather | bytes 17408 | tf_op jit(solution)/shard_map/all_gather | solution.py:98
  104.4 10.5 %all-gather.12.cloned.1.call-done = bf16[2048,768]{1,0:T(8,128)(2,1)} async-done(((bf16[128,768]{1,0:T(8,128)(2,1)}), bf16[2048,768]{1,0:T(8,128)(2,1)}) %all-gather.12.cloned.1.call-update) | async-done | bytes 3145744 | tf_op jit(solution)/shard_map/all_gather | solution.py:158
  114.9 2.8 fusion.257
  118.5 19.6 %all-gather.14.cloned.1.call-done = bf16[768,768]{1,0:T(8,128)(2,1)} async-done(((bf16[768,384]{1,0:T(8,128)(2,1)}), bf16[768,768]{1,0:T(8,128)(2,1)}) %all-gather.14.cloned.1.call-update) | async-done | bytes 1179664 | tf_op jit(solution)/shard_map/all_gather | solution.py:99
  138.1 7.5 %fusion.259 = f32[2048,768]{0,1:T(8,128)} fusion(bf16[2048,768]{1,0:T(8,128)(2,1)} %all-gather.12.cloned.1.call-done, bf16[768,768]{1,0:T(8,128)(2,1)} %all-gather.14.cloned.1.call-done), kind=kOutput, calls=%fused_computation.499 | convolution fusion | flops 2415919104 | bytes 10616832 | tf_op jit(solution)/shard_map/dot_general | solution.py:40
  145.6 16.7 %all-gather.16.cloned.1.call-done = bf16[768,768]{1,0:T(8,128)(2,1)} async-done(((bf16[768,384]{1,0:T(8,128)(2,1)}), bf16[768,768]{1,0:T(8,128)(2,1)}) %all-gather.16.cloned.1.call-update) | async-done | bytes 1179664 | tf_op jit(solution)/shard_map/all_gather | solution.py:105
  162.3 47.4 %all-gather.20.cloned.1.call-done = bf16[1,2048,768]{2,1,0:T(8,128)(2,1)} async-done(((bf16[1,128,768]{2,1,0:T(8,128)(2,1)}), bf16[1,2048,768]{2,1,0:T(8,128)(2,1)}) %all-gather.20.cloned.1.call-update) | async-done | bytes 3145744 | tf_op jit(solution)/shard_map/all_gather | solution.py:108
  209.7 15.3 %select_reduce_fusion.3 = (f32[2048]{0:T(1024)}, f32[2048]{0:T(1024)}, f32[2048]{0:T(1024)}, f32[2048]{0:T(1024)}, bf16[2048,768]{0,1:T(8,128)(2,1)}, /*index=5*/bf16[2048,768]{0,1:T(8,128)(2,1)S(1)}) fusion(pred[768]{0:T(1024)(128)(4,1)} %get-tuple-element.174, pred[768]{0:T(1024)(128)(4,1)} %get-tuple-element.175, pred[768]{0:T(1024)(128)(4,1)} %get-tuple-element.170, ...), kind=kOutput, calls=%fused_computation.16 | convolution fusion | flops 2472534016 | bytes 16979200 | tf_op jit(solution)/shard_map/dot_general | solution.py:40
  225.0 1.7 copy-done.90
  226.7 4.1 convolution_convert_fusion
  249.6 7.5 %convolution_convert_fusion.1 = bf16[2048,768]{1,0:T(8,128)(2,1)} fusion(bf16[768,768]{1,0:T(8,128)(2,1)} %all-gather.16.cloned.1.call-done, bf16[2048,768]{0,1:T(8,128)(2,1)} %get-tuple-element.126, f32[2048]{0:T(1024)S(1)} %bitcast.258, f32[2048]{0:T(1024)} %bitcast.261, f32[2048]{0:T(1024)} %bitcast.264, f32[2048]{0:T(1024)S(1)} %bitcast.255, ...), kind=kOutput, calls=%fused_computation.20 | convolution fusion | flops 2426929152 | bytes 7506176 | tf_op jit(solution)/shard_map/dot_general | solution.py:40
  263.6 6.3 %fusion.10 = f32[768,768]{1,0:T(8,128)S(1)} fusion(bf16[1,2048,768]{2,1,0:T(8,128)(2,1)} %all-gather.20.cloned.1.call-done, bf16[2048,768]{0,1:T(8,128)(2,1)} %get-tuple-element.126, f32[2048]{0:T(1024)} %bitcast.259, f32[2048]{0:T(1024)} %bitcast.262, f32[2048]{0:T(1024)} %bitcast.265, f32[2048]{0:T(1024)} %bitcast.256, ...), kind=kOutput, calls=%fused_computation.23 | convolution fusion | flops 2425356288 | bytes 8685824 | tf_op jit(solution)/shard_map/dot_general | solution.py:40
  270.9 1.6 collective-permute-start.4
  272.4 2.6 fusion.260
  277.9 60.6 %all-reduce = f32[16,512]{1,0:T(8,128)} all-reduce(f32[16,512]{1,0:T(8,128)} %bitcast.247), channel_id=7, replica_groups=mesh['fsdp'=2,'ctx'=4,'tp'=4] {'ctx','tp'}, use_global_device_ids=true, to_apply=%region_14.15.clone | all-reduce | flops 8192 | bytes 65536
  341.0 1.8 fusion.245
  344.1 2.7 convert_add_fusion
  346.8 2.2 convert_add_fusion.1
  349.1 2.8 multiply_reduce_fusion.1
  351.8 13.3 %reduce-scatter.6.cloned.1.call-done = bf16[128,768]{1,0:T(8,128)(2,1)} async-done(((bf16[2048,768]{1,0:T(8,128)(2,1)}), bf16[128,768]{1,0:T(8,128)(2,1)}) %reduce-scatter.6.cloned.1.call-update) | async-done | bytes 196624 | tf_op jit(solution)/shard_map/reduce_scatter | solution.py:193
  365.1 2.3 fusion.252
  367.4 8.1 %all_gather.45 = bf16[512,768]{1,0:T(8,128)(2,1)S(1)} all-gather(bf16[128,768]{1,0:T(8,128)(2,1)S(1)} %get-tuple-element.124), channel_id=1, replica_groups=mesh['fsdp'=2,'ctx'=4,'tp'=4] {'ctx'}, dimensions={0}, use_global_device_ids=true | all-gather | bytes 983040 | tf_op jit(solution)/shard_map/all_gather | solution.py:220
  377.8 1.4 multiply_reduce_fusion
  379.2 2.7 multiply_convert_fusion.1
  384.2 4.5 convolution_convert_fusion.5
  389.1 1.9 convolution_convert_fusion.2
  391.4 1.5 copy.101
  393.2 1.6 select_reduce_fusion.4
  395.8 1.4 select_reduce_fusion.40
  398.8 57.7 %reduce-scatter.10.cloned.1.call-done = bf16[96,768]{1,0:T(8,128)(2,1)} async-done(((bf16[768,768]{1,0:T(8,128)(2,1)}), bf16[96,768]{1,0:T(8,128)(2,1)}) %reduce-scatter.10.cloned.1.call-update) | async-done | bytes 147472 | tf_op jit(solution)/shard_map/reduce_scatter | solution.py:247
  459.5 1.8 fusion.31
  462.6 1.5 collective-permute-start.1
  466.0 3.9 collective-permute-done
  469.8 2.1 collective-permute-done.1
  472.0 2.6 collective-permute-done.2
  475.8 74.3 %all_gather.46 = f32[32,39,128]{2,1,0:T(8,128)S(1)} all-gather(f32[1,39,128]{2,1,0:T(8,128)S(1)} %maximum_bitcast_fusion), channel_id=1, replica_groups=mesh['fsdp'=2,'ctx'=4,'tp'=4] {'fsdp','ctx','tp'}, dimensions={0}, use_global_device_ids=true | all-gather | bytes 658944 | tf_op jit(solution)/shard_map/all_gather | solution.py:16
  553.2 2.1 convert.13
  555.3 1.9 slice_bitcast_fusion.1
  557.7 1.5 copy.96
  559.1 4.7 concatenate.45
  (403 shorter events, 64.4 us)
Async XLA Ops:
  7.2 24.8 %copy-start.86 = (bf16[384]{0:T(512)(128)(2,1)S(1)}, bf16[384]{0:T(512)(128)(2,1)}, u32[]{:S(2)}) copy-start(bf16[384]{0:T(512)(128)(2,1)} %param.15) | copy-start | bytes 2308
  7.2 24.8 %copy-start.87 = (bf16[384]{0:T(512)(128)(2,1)S(1)}, bf16[384]{0:T(512)(128)(2,1)}, u32[]{:S(2)}) copy-start(bf16[384]{0:T(512)(128)(2,1)} %param.19) | copy-start | bytes 2308
  7.2 24.8 %copy-start.82 = (bf16[384,4]{0,1:T(4,128)(2,1)S(1)}, bf16[384,4]{0,1:T(4,128)(2,1)}, u32[]{:S(2)}) copy-start(bf16[384,4]{0,1:T(4,128)(2,1)} %param.20) | copy-start | bytes 9220
  7.2 30.3 %copy-start.6 = (bf16[1,128,768]{2,1,0:T(8,128)(2,1)S(1)}, bf16[1,128,768]{2,1,0:T(8,128)(2,1)}, u32[]{:S(2)}) copy-start(bf16[1,128,768]{2,1,0:T(8,128)(2,1)} %param.12) | copy-start | bytes 589828
  7.2 57.8 %all-gather.10.cloned.1.call-start = ((), (), s32[]{:S(2)}) async-start(), calls=%async_computation.4 | async-start | bytes 1769472 | tf_op jit(solution)/shard_map/all_gather | solution.py:97
  8.0 107.0 %all-gather.12.cloned.1.call-start = ((), (), s32[]{:S(2)}) async-start(), calls=%async_computation.5 | async-start | bytes 3342336 | tf_op jit(solution)/shard_map/all_gather | solution.py:158
  9.2 37.1 %copy-start.71 = (s32[1,512]{1,0:T(1,128)S(1)}, s32[1,512]{1,0:T(1,128)}, u32[]{:S(2)}) copy-start(s32[1,512]{1,0:T(1,128)} %param.13) | copy-start | bytes 6148
  32.0 16.8 %copy-start.15 = (bf16[768,576]{1,0:T(8,128)(2,1)}, bf16[768,576]{1,0:T(8,128)(2,1)S(1)}, u32[]{:S(2)}) copy-start(bf16[768,576]{1,0:T(8,128)(2,1)S(1)} %all_gather.38) | copy-start | bytes 2654212
  37.6 11.2 %copy-start.64 = (f32[768]{0:T(1024)}, f32[768]{0:T(1024)S(1)}, u32[]{:S(2)}) copy-start(f32[768]{0:T(1024)S(1)} %get-tuple-element.88) | copy-start | bytes 9220
  37.6 29.9 %copy-start.25 = (f32[768]{0:T(1024)}, f32[768]{0:T(1024)S(1)}, u32[]{:S(2)}) copy-start(f32[768]{0:T(1024)S(1)} %get-tuple-element.87) | copy-start | bytes 9220
  51.6 326.1 %copy-start.2 = (f32[3,512,512]{1,2,0:T(8,128)}, f32[3,512,512]{1,2,0:T(8,128)S(1)}, u32[]{:S(2)}) copy-start(f32[3,512,512]{1,2,0:T(8,128)S(1)} %get-tuple-element.160) | copy-start | bytes 9437188
  56.5 8.5 %copy-start.17 = (bf16[3,64,512]{2,1,0:T(8,128)(2,1)}, bf16[3,64,512]{2,1,0:T(8,128)(2,1)S(1)}, u32[]{:S(2)}) copy-start(bf16[3,64,512]{2,1,0:T(8,128)(2,1)S(1)} %convolution_convert_fusion.6) | copy-start | bytes 589828
  56.5 13.7 %copy-start.80 = (s32[1,128,2]{1,2,0:T(2,128)S(1)}, s32[1,128,2]{1,2,0:T(2,128)}, u32[]{:S(2)}) copy-start(s32[1,128,2]{1,2,0:T(2,128)} %param.14) | copy-start | bytes 3076
  67.4 37.0 %copy-start.79 = (f32[128]{0:T(128)}, f32[128]{0:T(128)S(1)}, u32[]{:S(2)}) copy-start(f32[128]{0:T(128)S(1)} %get-tuple-element.158) | copy-start | bytes 1540
  68.3 69.9 %all-gather.14.cloned.1.call-start = ((), (), s32[]{:S(2)}) async-start(), calls=%async_computation.6 | async-start | bytes 1769472 | tf_op jit(solution)/shard_map/all_gather | solution.py:99
  69.0 93.3 %all-gather.16.cloned.1.call-start = ((), (), s32[]{:S(2)}) async-start(), calls=%async_computation.7 | async-start | bytes 1769472 | tf_op jit(solution)/shard_map/all_gather | solution.py:105
  69.6 140.1 %all-gather.20.cloned.1.call-start = ((), (), s32[]{:S(2)}) async-start(), calls=%async_computation.11 | async-start | bytes 3342336 | tf_op jit(solution)/shard_map/all_gather | solution.py:108
  70.2 278.9 %reduce-scatter.8.cloned.1.call-start = ((), (), s32[]{:S(2)}) async-start(), calls=%async_computation.9 | async-start | bytes 3342336 | tf_op jit(solution)/shard_map/reduce_scatter | solution.py:190
  118.5 131.1 %copy-start.72 = (f32[2048,1]{0,1:T(1,128)}, f32[2048,1]{0,1:T(1,128)S(1)}, u32[]{:S(2)}) copy-start(f32[2048,1]{0,1:T(1,128)S(1)} %get-tuple-element.147) | copy-start | bytes 24580
  118.5 131.1 %copy-start.73 = (f32[2048,1]{0,1:T(1,128)}, f32[2048,1]{0,1:T(1,128)S(1)}, u32[]{:S(2)}) copy-start(f32[2048,1]{0,1:T(1,128)S(1)} %get-tuple-element.148) | copy-start | bytes 24580
  209.7 17.0 %copy-start.89 = (bf16[768,768]{1,0:T(8,128)(2,1)S(1)}, bf16[768,768]{1,0:T(8,128)(2,1)}, u32[]{:S(2)}) copy-start(bf16[768,768]{1,0:T(8,128)(2,1)} %all-gather.14.cloned.1.call-done) | copy-start | bytes 3538948
  230.8 134.4 %reduce-scatter.6.cloned.1.call-start = ((), (), s32[]{:S(2)}) async-start(), calls=%async_computation.8 | async-start | bytes 3342336 | tf_op jit(solution)/shard_map/reduce_scatter | solution.py:193
  257.1 199.4 %reduce-scatter.10.cloned.1.call-start = ((), (), s32[]{:S(2)}) async-start(), calls=%async_computation.12 | async-start | bytes 1327104 | tf_op jit(solution)/shard_map/reduce_scatter | solution.py:247
  261.8 8.0 %copy-start.68 = (s32[128]{0:T(128)}, s32[128]{0:T(128)S(1)}, u32[]{:S(2)}) copy-start(s32[128]{0:T(128)S(1)} %get-tuple-element.154) | copy-start | bytes 1540
  262.9 6.9 %copy-start.70 = (f32[128]{0:T(128)}, f32[128]{0:T(128)S(1)}, u32[]{:S(2)}) copy-start(f32[128]{0:T(128)S(1)} %get-tuple-element.165) | copy-start | bytes 1540
  263.6 8.9 %copy-start.3 = (bf16[2048,768]{1,0:T(8,128)(2,1)S(1)}, bf16[2048,768]{1,0:T(8,128)(2,1)}, u32[]{:S(2)}) copy-start(bf16[2048,768]{1,0:T(8,128)(2,1)} %all-gather.12.cloned.1.call-done) | copy-start | bytes 9437188
  263.6 8.9 %copy-start.91 = (bf16[2048,768]{0,1:T(8,128)(2,1)S(1)}, bf16[2048,768]{0,1:T(8,128)(2,1)}, u32[]{:S(2)}) copy-start(bf16[2048,768]{0,1:T(8,128)(2,1)} %copy-done.90) | copy-start | bytes 9437188
  270.8 6.4 %copy-start.74 = (f32[2048]{0:T(1024)S(1)}, f32[2048]{0:T(1024)}, u32[]{:S(2)}) copy-start(f32[2048]{0:T(1024)} %get-tuple-element.10) | copy-start | bytes 24580
  270.8 6.4 %copy-start.75 = (f32[2048]{0:T(1024)S(1)}, f32[2048]{0:T(1024)}, u32[]{:S(2)}) copy-start(f32[2048]{0:T(1024)} %get-tuple-element.11) | copy-start | bytes 24580
  270.8 6.4 %copy-start.76 = (f32[2048]{0:T(1024)S(1)}, f32[2048]{0:T(1024)}, u32[]{:S(2)}) copy-start(f32[2048]{0:T(1024)} %get-tuple-element.12) | copy-start | bytes 24580
  270.8 6.4 %copy-start.77 = (f32[2048]{0:T(1024)S(1)}, f32[2048]{0:T(1024)}, u32[]{:S(2)}) copy-start(f32[2048]{0:T(1024)} %get-tuple-element.13) | copy-start | bytes 24580
  270.9 73.3 %collective-permute-start.4 = (bf16[768,384]{1,0:T(8,128)(2,1)}, bf16[768,384]{1,0:T(8,128)(2,1)}, u32[]{:S(2)}, u32[]{:S(2)}) collective-permute-start(bf16[768,384]{1,0:T(8,128)(2,1)} %dynamic-slice_convert_fusion), channel_id=1, source_target_pairs={{0,16},{16,0},{1,17},{17,1},{2,18},{18,2},{3,19},{19,3},{4,20},{20... | collective-permute-start | bytes 1769480 | tf_op jit(solution)/shard_map/ppermute | solution.py:51
  276.7 70.1 %collective-permute-start.3 = (bf16[768,384]{1,0:T(8,128)(2,1)}, bf16[768,384]{1,0:T(8,128)(2,1)}, u32[]{:S(2)}, u32[]{:S(2)}) collective-permute-start(bf16[768,384]{1,0:T(8,128)(2,1)} %dynamic-slice_convert_fusion.1), channel_id=1, source_target_pairs={{0,16},{16,0},{1,17},{17,1},{2,18},{18,2},{3,19},{19,3},{4,20},{20... | collective-permute-start | bytes 1769480 | tf_op jit(solution)/shard_map/ppermute | solution.py:51
  277.3 71.8 %copy-start.26 = (f32[768]{0:T(1024)S(1)}, f32[768]{0:T(1024)}, u32[]{:S(2)}) copy-start(f32[768]{0:T(1024)} %copy-done.25) | copy-start | bytes 9220
  365.1 12.6 %copy-start.21 = (bf16[512,576]{0,1:T(8,128)(2,1)S(1)}, bf16[512,576]{0,1:T(8,128)(2,1)}, u32[]{:S(2)}) copy-start(bf16[512,576]{0,1:T(8,128)(2,1)} %copy-done.20) | copy-start | bytes 1769476
  391.3 68.1 %copy-start.23 = (bf16[3,64,512]{2,1,0:T(8,128)(2,1)S(1)}, bf16[3,64,512]{2,1,0:T(8,128)(2,1)}, u32[]{:S(2)}) copy-start(bf16[3,64,512]{2,1,0:T(8,128)(2,1)} %fusion.17) | copy-start | bytes 589828
  391.4 68.1 %copy-start.24 = (bf16[3,64,512]{2,1,0:T(8,128)(2,1)S(1)}, bf16[3,64,512]{2,1,0:T(8,128)(2,1)}, u32[]{:S(2)}) copy-start(bf16[3,64,512]{2,1,0:T(8,128)(2,1)} %fusion.18) | copy-start | bytes 589828
  392.9 66.6 %copy-start.16 = (bf16[768,576]{1,0:T(8,128)(2,1)S(1)}, bf16[768,576]{1,0:T(8,128)(2,1)}, u32[]{:S(2)}) copy-start(bf16[768,576]{1,0:T(8,128)(2,1)} %copy-done.15) | copy-start | bytes 2654212
  392.9 160.2 %all-gather.18.cloned.1.call-start = ((), (), s32[]{:S(2)}) async-start(), calls=%async_computation.10 | async-start | bytes 2506752 | tf_op jit(solution)/shard_map/all_gather | solution.py:250
  395.8 78.8 %copy-start.7 = (bf16[1,128,768]{2,1,0:T(8,128)(2,1)S(1)}, bf16[1,128,768]{2,1,0:T(8,128)(2,1)}, u32[]{:S(2)}) copy-start(bf16[1,128,768]{2,1,0:T(8,128)(2,1)} %param.12) | copy-start | bytes 589828
  395.8 78.8 %copy-start.83 = (f32[128]{0:T(128)S(1)}, f32[128]{0:T(128)}, u32[]{:S(2)}) copy-start(f32[128]{0:T(128)} %get-tuple-element.156) | copy-start | bytes 1540
  459.5 16.3 %copy-start.63 = (f32[3072]{0:T(1024)S(1)}, f32[3072]{0:T(1024)}, u32[]{:S(2)}) copy-start(f32[3072]{0:T(1024)} %reshape.1326) | copy-start | bytes 36868
  459.5 16.3 %copy-start.69 = (f32[768]{0:T(1024)S(1)}, f32[768]{0:T(1024)}, u32[]{:S(2)}) copy-start(f32[768]{0:T(1024)} %get-tuple-element.17) | copy-start | bytes 9220
  459.5 92.8 %copy-start.11 = (f32[128,768]{1,0:T(8,128)S(1)}, f32[128,768]{1,0:T(8,128)}, u32[]{:S(2)}) copy-start(f32[128,768]{1,0:T(8,128)} %get-tuple-element.125) | copy-start | bytes 1179652
  459.5 92.8 %copy-start.88 = (f32[128]{0:T(128)S(1)}, f32[128]{0:T(128)}, u32[]{:S(2)}) copy-start(f32[128]{0:T(128)} %get-tuple-element.155) | copy-start | bytes 1540
  462.5 7.3 %collective-permute-start = (bf16[128,768]{1,0:T(8,128)(2,1)S(1)}, bf16[128,768]{1,0:T(8,128)(2,1)S(1)}, u32[]{:S(2)}, u32[]{:S(2)}) collective-permute-start(bf16[128,768]{1,0:T(8,128)(2,1)S(1)} %get-tuple-element.143), channel_id=1, source_target_pairs={{0,4},{4,8},{8,12},{12,0},{1,5},{5,9},{9,13},{13,1},{2,6},{6,10},{... | collective-permute-start | bytes 589832 | tf_op jit(solution)/shard_map/ppermute | solution.py:51
  462.6 9.4 %collective-permute-start.1 = (bf16[128,768]{1,0:T(8,128)(2,1)S(1)}, bf16[128,768]{1,0:T(8,128)(2,1)S(1)}, u32[]{:S(2)}, u32[]{:S(2)}) collective-permute-start(bf16[128,768]{1,0:T(8,128)(2,1)S(1)} %get-tuple-element.145), channel_id=1, source_target_pairs={{0,8},{4,12},{8,0},{12,4},{1,9},{5,13},{9,1},{13,5},{2,10},{6,14},... | collective-permute-start | bytes 589832 | tf_op jit(solution)/shard_map/ppermute | solution.py:51
  464.1 10.4 %collective-permute-start.2 = (bf16[128,768]{1,0:T(8,128)(2,1)S(1)}, bf16[128,768]{1,0:T(8,128)(2,1)S(1)}, u32[]{:S(2)}, u32[]{:S(2)}) collective-permute-start(bf16[128,768]{1,0:T(8,128)(2,1)S(1)} %get-tuple-element.144), channel_id=1, source_target_pairs={{0,12},{4,0},{8,4},{12,8},{1,13},{5,1},{9,5},{13,9},{2,14},{6,2},{... | collective-permute-start | bytes 589832 | tf_op jit(solution)/shard_map/ppermute | solution.py:51
  (58 other events, 196.9 us)
Sparse Core Ops, SparseCore 0:
  9.6 29.6 all-gather.9
  68.4 46.5 all-gather.11
  116.5 21.5 all-gather.13
  139.5 22.7 all-gather.15
  164.5 45.1 all-gather.19
  230.9 65.0 reduce-scatter.7
  299.8 65.2 reduce-scatter.5
  393.1 63.3 reduce-scatter.9
  458.8 42.7 all-gather.17
